TPU v7x, 512 devices: a whole 4x4x16 slice. The times are simulated.
512 devices in a mesh: ctx: 16 (over x_lo, y, core), dp: 32 (over x_hi, z).
Axes of the slice: x: 4 (x_hi: 2, x_lo: 2; x = x_hi * 2 + x_lo), y: 4, z: 16, core: 2. Of those that a mesh axis runs over, the one named last changes fastest.
Arguments:
- token_ids: int32 [32, 2048], P('dp', 'ctx'), may hold values from 0 to 511
- feature_table: bfloat16 [3072, 512], replicated, may hold values from -6 to 6
- short_weight: float32 [3072, 7], replicated, may hold values from -3 to 3
- residue: float32 [1024, 16], replicated, may hold values from -0.09375 to 0.09375
- rates: float32 [16], replicated, may hold values from 0.3 to 64
- skip_gain: float32 [1024], replicated, may hold values from 0.5 to 1.5
- grad_out: bfloat16 [32, 1024, 2048], P('dp', None, 'ctx'), may hold values from -0.0029296875 to 0.0029296875
Outputs:
- mixed: bfloat16 [32, 1024, 2048], P('dp', None, 'ctx')
- grad_residue: float32 [1024, 16], replicated
- grad_rate: float32 [16], replicated
All inputs are finite; a program needn't handle non-finite values.
Results may differ from a plain program's by a relative error of at most 0.0065.
Values may be sent and summed in bfloat16 or wider, within the bound.
A program may use at most 64 MiB of HBM per device.

v0:
```python
import math

import jax
import jax.numpy as jnp
from jax import lax
from jax.sharding import PartitionSpec as P

HIGHEST = lax.Precision.HIGHEST


def from_behind(block, axis, distance):
    devices = range(lax.axis_size(axis))
    route = [((i - distance) % len(devices), i) for i in devices]
    return lax.ppermute(block, axis, route)


def split_table(table):
    upper = table.astype(jnp.bfloat16)
    lower = (table - upper.astype(jnp.float32)).astype(jnp.bfloat16)
    return (upper, lower)


def split_dot(data, halves):
    return jnp.dot(data, halves[0], preferred_element_type=jnp.float32) + jnp.dot(
        data, halves[1], preferred_element_type=jnp.float32
    )


def dft_tables(block_len):
    period = 2 * block_len
    sample = jnp.arange(period, dtype=jnp.int32)[:, None]
    harmonic = jnp.arange(block_len, dtype=jnp.int32)[None, :]
    phase = (sample * harmonic % period).astype(jnp.float32) * (2.0 * math.pi / period)
    parity = 1.0 - 2.0 * (sample % 2).astype(jnp.float32)
    forward = jnp.concatenate(
        [jnp.cos(phase), jnp.where(harmonic == 0, parity, -jnp.sin(phase))], axis=1
    )
    outputs = block_len + jnp.arange(block_len, dtype=jnp.int32)[None, :]
    column = jnp.arange(block_len, dtype=jnp.int32)[:, None]
    angle = (column * outputs % period).astype(jnp.float32) * (2.0 * math.pi / period)
    leading = column == 0
    real_rows = jnp.where(leading, 1.0, 2.0) / period * jnp.cos(angle)
    out_parity = (1.0 - 2.0 * (outputs % 2).astype(jnp.float32)) / period
    imag_rows = jnp.where(leading, out_parity, -2.0 / period * jnp.sin(angle))
    inverse = jnp.concatenate([real_rows, imag_rows], axis=0)
    parseval = jnp.where(jnp.arange(period) % block_len == 0, 1.0, 2.0) / period
    return (forward, inverse, parseval)


def packed_product(left, right, conjugate):
    half = left.shape[-1] // 2
    left_re = left[..., :half]
    left_im = left[..., half:]
    right_re = right[..., :half]
    right_im = right[..., half:]
    leading = jnp.arange(half) == 0
    if conjugate:
        real_part = jnp.where(leading, left_re * right_re, left_re * right_re + left_im * right_im)
        imag_part = jnp.where(leading, left_im * right_im, left_re * right_im - left_im * right_re)
    else:
        real_part = jnp.where(leading, left_re * right_re, left_re * right_re - left_im * right_im)
        imag_part = jnp.where(leading, left_im * right_im, left_re * right_im + left_im * right_re)
    return jnp.concatenate([real_part, imag_part], axis=-1)


def per_device(token_ids, feature_table, short_weight, residue, rates, skip_gain, grad_out):
    block_len = token_ids.shape[1]
    blocks = lax.axis_size("ctx")
    own_index = lax.axis_index("ctx")
    seq_len = block_len * blocks
    channels = residue.shape[0]
    modes = residue.shape[1]
    vocab_size = feature_table.shape[1]
    taps_short = short_weight.shape[1]
    ids_row = token_ids[0]
    previous = from_behind(ids_row[block_len - (taps_short - 1) :], "ctx", 1)
    vocab_column = jnp.arange(vocab_size, dtype=jnp.int32)[:, None]
    onehot_own = (vocab_column == ids_row[None, :]).astype(jnp.bfloat16)
    onehot_prev = (vocab_column == previous[None, :]).astype(jnp.bfloat16)
    feature_own = jnp.dot(feature_table, onehot_own, preferred_element_type=jnp.float32)
    feature_prev = jnp.dot(feature_table, onehot_prev, preferred_element_type=jnp.float32)
    padded = jnp.concatenate([feature_prev, feature_own], axis=1)
    mixer = jnp.zeros(feature_own.shape, jnp.float32)
    for offset in range(taps_short):
        mixer = (
            mixer + short_weight[:, offset : offset + 1] * padded[:, offset : offset + block_len]
        )
    queries = mixer[:channels]
    gated = (mixer[channels : 2 * channels] * mixer[2 * channels :]).astype(jnp.bfloat16)
    gated_f = gated.astype(jnp.float32)
    forward, inverse, parseval = dft_tables(block_len)
    forward_low = split_table(forward[:block_len])
    forward_high = forward[block_len:]
    dconv = queries * grad_out[0].astype(jnp.float32)
    dconv_spec = jnp.dot(dconv, forward_high, precision=HIGHEST)
    sample = jnp.arange(2 * block_len, dtype=jnp.int32)
    mode_index = jnp.arange(modes, dtype=jnp.int32)[:, None] + 1
    period = 2 * modes + 2

    def mode_spectra(offset):
        delay = (offset * block_len - block_len + sample) % seq_len
        delay_f = delay.astype(jnp.float32)
        cycle_step = mode_index * delay[None, :] % period
        oscillation = jnp.cos(cycle_step.astype(jnp.float32) * (2.0 * math.pi / period))
        power = jnp.exp(-rates[:, None] * delay_f[None, :] / seq_len) * oscillation
        slope = power * (-delay_f[None, :] / seq_len)
        stacked = jnp.concatenate([power, slope], axis=0)
        return jnp.dot(stacked, forward, precision=HIGHEST)

    def pair_terms(block, source):
        offset = (own_index - source) % blocks
        block_spec = split_dot(block, forward_low)
        spectra = mode_spectra(offset)
        filt_spec = jnp.dot(residue, spectra[:modes], precision=HIGHEST)
        out_spec = packed_product(filt_spec, block_spec, False)
        cross_spec = packed_product(block_spec, dconv_spec, True) * parseval[None, :]
        grad_terms = jnp.dot(cross_spec, spectra.T, precision=HIGHEST)
        return (out_spec, grad_terms)

    def process(carry, block, source):
        out_spec, grad_terms = pair_terms(block, source)
        return (carry[0] + out_spec, carry[1] + grad_terms)

    start = (
        jnp.zeros((channels, 2 * block_len), jnp.float32),
        jnp.zeros((channels, 2 * modes), jnp.float32),
    )
    totals = process(start, gated, own_index)

    def loop_step(step, carry):
        moved = from_behind(carry[2], "ctx", 1)
        source = (own_index - step) % blocks
        summed = process((carry[0], carry[1]), moved, source)
        return (summed[0], summed[1], moved)

    result = lax.fori_loop(1, blocks, loop_step, (totals[0], totals[1], gated))
    totals = (result[0], result[1])
    conv = jnp.dot(totals[0], inverse, precision=HIGHEST)
    mixed = (queries * (conv + skip_gain[:, None] * gated_f)).astype(jnp.bfloat16)[None]
    grad_part = totals[1][:, :modes]
    rate_part = jnp.sum(residue * totals[1][:, modes:], axis=0)
    grad_residue, grad_rate = lax.psum((grad_part, rate_part), ("ctx", "dp"))
    return (mixed, grad_residue, grad_rate)


def solution(mesh):
    return jax.shard_map(
        per_device,
        mesh=mesh,
        in_specs=(P("dp", "ctx"), P(), P(), P(), P(), P(), P("dp", None, "ctx")),
        out_specs=(P("dp", None, "ctx"), P(), P()),
        check_vma=False,
    )
```

profile of v0, /device:TPU:1, one launch (start us, length us, event | category | flops | bytes accessed | tf_op | source)
XLA Modules:
  0.0 718.3 jit_solution(9013553450045203763)
XLA Ops:
  8.6 4.6 collective-permute-start.1
  17.0 2.1 fusion.108
  22.6 2.0 convolution_bitcast_fusion.3
  31.9 2.1 fusion.50
  38.2 218.4 %while.21 = (s32[]{:T(128)}, f32[1024,256]{0,1:T(8,128)}, f32[1024,32]{0,1:T(8,128)S(1)}, bf16[1024,128]{1,0:T(8,128)(2,1)}, f32[16,1]{0,1:T(1,128)S(1)}, /*inde...) while((s32[]{:T(128)}, f32[1024,256]{0,1:T(8,128)}, ...), condition=%wide.region_1.2_spmd.clone, body=%wide.region_0.1_spmd.clone.sunk | while | flops 313890176 | bytes 29451272 | solution.py:136
  43.5 2.1 collective-permute-done
  50.3 2.5 collective-permute-start
  56.1 4.2 collective-permute-done
  70.3 4.7 collective-permute-done
  85.0 4.7 collective-permute-done
  99.8 4.7 collective-permute-done
  114.5 4.7 collective-permute-done
  129.2 4.7 collective-permute-done
  144.0 4.7 collective-permute-done
  158.7 4.7 collective-permute-done
  173.4 4.7 collective-permute-done
  188.2 4.7 collective-permute-done
  202.9 4.7 collective-permute-done
  217.7 4.7 collective-permute-done
  232.4 4.7 collective-permute-done
  247.1 4.7 collective-permute-done
  258.2 2.2 fusion.45
  260.5 109.2 %psum.15 = f32[16]{0:T(128)} all-reduce(f32[16]{0:T(128)S(1)} %get-tuple-element.467), channel_id=1, replica_groups=mesh['ctx'=16,'dp'=32] {'ctx','dp'}, use_global_device_ids=true, to_apply=%region_4.5 | all-reduce | flops 16 | bytes 128 | tf_op jit(solution)/shard_map/psum | solution.py:142
  370.5 339.5 %all-reduce.2.cloned.1.call-done = f32[1024,16]{0,1:T(8,128)} async-done(((f32[1024,16]{0,1:T(8,128)}), f32[1024,16]{0,1:T(8,128)}) %all-reduce.2.cloned.1.call-update) | async-done | bytes 65552 | tf_op jit(solution)/shard_map/psum | solution.py:142
  (429 shorter events, 169.2 us)
Async XLA Ops:
  7.2 13.7 %copy-start = (bf16[3072,512]{1,0:T(8,128)(2,1)S(1)}, bf16[3072,512]{1,0:T(8,128)(2,1)}, u32[]{:S(2)}) copy-start(bf16[3072,512]{1,0:T(8,128)(2,1)} %param.10) | copy-start | bytes 9437188
  7.2 13.7 %copy-start.25 = (s32[1,128]{1,0:T(1,128)S(1)}, s32[1,128]{1,0:T(1,128)}, u32[]{:S(2)}) copy-start(s32[1,128]{1,0:T(1,128)} %param.9) | copy-start | bytes 1540
  7.2 13.7 %copy-start.29 = (f32[16]{0:T(128)S(1)}, f32[16]{0:T(128)}, u32[]{:S(2)}) copy-start(f32[16]{0:T(128)} %param.13) | copy-start | bytes 196
  7.2 702.8 %all-reduce.2.cloned.1.call-start = ((), (), s32[]{:S(2)}) async-start(), calls=%async_computation | async-start | bytes 131072 | tf_op jit(solution)/shard_map/psum | solution.py:142
  8.6 17.0 %collective-permute-start.1 = (s32[6]{0:T(128)}, s32[6]{0:T(128)}, u32[]{:S(2)}, u32[]{:S(2)}) collective-permute-start(s32[6]{0:T(128)} %slice_bitcast_fusion), channel_id=1, source_target_pairs={{480,0},{0,32},{32,64},{64,96},{96,128},{128,160},{160,192},{192,2... | collective-permute-start | bytes 80 | tf_op jit(solution)/shard_map/ppermute | solution.py:14
  38.2 220.0 %copy-start.23 = (f32[1024]{0:T(1024)S(1)}, f32[1024]{0:T(1024)}, u32[]{:S(2)}) copy-start(f32[1024]{0:T(1024)} %param.14) | copy-start | bytes 12292
  38.2 7.3 %collective-permute-start = (bf16[1024,128]{1,0:T(8,128)(2,1)}, bf16[1024,128]{1,0:T(8,128)(2,1)S(1)}, u32[]{:S(2)}, u32[]{:S(2)}) collective-permute-start(bf16[1024,128]{1,0:T(8,128)(2,1)} %get-tuple-element.591), channel_id=1, source_target_pairs={{480,0},{0,32},{32,64},{64,96},{96,128},{128,160},{160,192},{192,2... | collective-permute-start | bytes 786440 | tf_op jit(solution)/shard_map/while/body/eval_jaxpr/ppermute | solution.py:14
  50.3 10.0 %collective-permute-start = (bf16[1024,128]{1,0:T(8,128)(2,1)}, bf16[1024,128]{1,0:T(8,128)(2,1)S(1)}, u32[]{:S(2)}, u32[]{:S(2)}) collective-permute-start(bf16[1024,128]{1,0:T(8,128)(2,1)} %get-tuple-element.591), channel_id=1, source_target_pairs={{480,0},{0,32},{32,64},{64,96},{96,128},{128,160},{160,192},{192,2... | collective-permute-start | bytes 786440 | tf_op jit(solution)/shard_map/while/body/eval_jaxpr/ppermute | solution.py:14
  65.0 10.0 %collective-permute-start = (bf16[1024,128]{1,0:T(8,128)(2,1)}, bf16[1024,128]{1,0:T(8,128)(2,1)S(1)}, u32[]{:S(2)}, u32[]{:S(2)}) collective-permute-start(bf16[1024,128]{1,0:T(8,128)(2,1)} %get-tuple-element.591), channel_id=1, source_target_pairs={{480,0},{0,32},{32,64},{64,96},{96,128},{128,160},{160,192},{192,2... | collective-permute-start | bytes 786440 | tf_op jit(solution)/shard_map/while/body/eval_jaxpr/ppermute | solution.py:14
  79.8 10.0 %collective-permute-start = (bf16[1024,128]{1,0:T(8,128)(2,1)}, bf16[1024,128]{1,0:T(8,128)(2,1)S(1)}, u32[]{:S(2)}, u32[]{:S(2)}) collective-permute-start(bf16[1024,128]{1,0:T(8,128)(2,1)} %get-tuple-element.591), channel_id=1, source_target_pairs={{480,0},{0,32},{32,64},{64,96},{96,128},{128,160},{160,192},{192,2... | collective-permute-start | bytes 786440 | tf_op jit(solution)/shard_map/while/body/eval_jaxpr/ppermute | solution.py:14
  81.7 9.3 %copy-start.10 = (bf16[128,256]{1,0:T(8,128)(2,1)S(1)}, bf16[128,256]{1,0:T(8,128)(2,1)}, u32[]{:S(2)}) copy-start(bf16[128,256]{1,0:T(8,128)(2,1)} %get-tuple-element.613) | copy-start | bytes 196612 | tf_op jit(solution)/shard_map/while
  94.5 10.0 %collective-permute-start = (bf16[1024,128]{1,0:T(8,128)(2,1)}, bf16[1024,128]{1,0:T(8,128)(2,1)S(1)}, u32[]{:S(2)}, u32[]{:S(2)}) collective-permute-start(bf16[1024,128]{1,0:T(8,128)(2,1)} %get-tuple-element.591), channel_id=1, source_target_pairs={{480,0},{0,32},{32,64},{64,96},{96,128},{128,160},{160,192},{192,2... | collective-permute-start | bytes 786440 | tf_op jit(solution)/shard_map/while/body/eval_jaxpr/ppermute | solution.py:14
  96.5 9.3 %copy-start.10 = (bf16[128,256]{1,0:T(8,128)(2,1)S(1)}, bf16[128,256]{1,0:T(8,128)(2,1)}, u32[]{:S(2)}) copy-start(bf16[128,256]{1,0:T(8,128)(2,1)} %get-tuple-element.613) | copy-start | bytes 196612 | tf_op jit(solution)/shard_map/while
  109.2 10.0 %collective-permute-start = (bf16[1024,128]{1,0:T(8,128)(2,1)}, bf16[1024,128]{1,0:T(8,128)(2,1)S(1)}, u32[]{:S(2)}, u32[]{:S(2)}) collective-permute-start(bf16[1024,128]{1,0:T(8,128)(2,1)} %get-tuple-element.591), channel_id=1, source_target_pairs={{480,0},{0,32},{32,64},{64,96},{96,128},{128,160},{160,192},{192,2... | collective-permute-start | bytes 786440 | tf_op jit(solution)/shard_map/while/body/eval_jaxpr/ppermute | solution.py:14
  124.0 10.0 %collective-permute-start = (bf16[1024,128]{1,0:T(8,128)(2,1)}, bf16[1024,128]{1,0:T(8,128)(2,1)S(1)}, u32[]{:S(2)}, u32[]{:S(2)}) collective-permute-start(bf16[1024,128]{1,0:T(8,128)(2,1)} %get-tuple-element.591), channel_id=1, source_target_pairs={{480,0},{0,32},{32,64},{64,96},{96,128},{128,160},{160,192},{192,2... | collective-permute-start | bytes 786440 | tf_op jit(solution)/shard_map/while/body/eval_jaxpr/ppermute | solution.py:14
  138.7 10.0 %collective-permute-start = (bf16[1024,128]{1,0:T(8,128)(2,1)}, bf16[1024,128]{1,0:T(8,128)(2,1)S(1)}, u32[]{:S(2)}, u32[]{:S(2)}) collective-permute-start(bf16[1024,128]{1,0:T(8,128)(2,1)} %get-tuple-element.591), channel_id=1, source_target_pairs={{480,0},{0,32},{32,64},{64,96},{96,128},{128,160},{160,192},{192,2... | collective-permute-start | bytes 786440 | tf_op jit(solution)/shard_map/while/body/eval_jaxpr/ppermute | solution.py:14
  153.5 10.0 %collective-permute-start = (bf16[1024,128]{1,0:T(8,128)(2,1)}, bf16[1024,128]{1,0:T(8,128)(2,1)S(1)}, u32[]{:S(2)}, u32[]{:S(2)}) collective-permute-start(bf16[1024,128]{1,0:T(8,128)(2,1)} %get-tuple-element.591), channel_id=1, source_target_pairs={{480,0},{0,32},{32,64},{64,96},{96,128},{128,160},{160,192},{192,2... | collective-permute-start | bytes 786440 | tf_op jit(solution)/shard_map/while/body/eval_jaxpr/ppermute | solution.py:14
  168.2 10.0 %collective-permute-start = (bf16[1024,128]{1,0:T(8,128)(2,1)}, bf16[1024,128]{1,0:T(8,128)(2,1)S(1)}, u32[]{:S(2)}, u32[]{:S(2)}) collective-permute-start(bf16[1024,128]{1,0:T(8,128)(2,1)} %get-tuple-element.591), channel_id=1, source_target_pairs={{480,0},{0,32},{32,64},{64,96},{96,128},{128,160},{160,192},{192,2... | collective-permute-start | bytes 786440 | tf_op jit(solution)/shard_map/while/body/eval_jaxpr/ppermute | solution.py:14
  170.1 9.3 %copy-start.10 = (bf16[128,256]{1,0:T(8,128)(2,1)S(1)}, bf16[128,256]{1,0:T(8,128)(2,1)}, u32[]{:S(2)}) copy-start(bf16[128,256]{1,0:T(8,128)(2,1)} %get-tuple-element.613) | copy-start | bytes 196612 | tf_op jit(solution)/shard_map/while
  182.9 10.0 %collective-permute-start = (bf16[1024,128]{1,0:T(8,128)(2,1)}, bf16[1024,128]{1,0:T(8,128)(2,1)S(1)}, u32[]{:S(2)}, u32[]{:S(2)}) collective-permute-start(bf16[1024,128]{1,0:T(8,128)(2,1)} %get-tuple-element.591), channel_id=1, source_target_pairs={{480,0},{0,32},{32,64},{64,96},{96,128},{128,160},{160,192},{192,2... | collective-permute-start | bytes 786440 | tf_op jit(solution)/shard_map/while/body/eval_jaxpr/ppermute | solution.py:14
  197.7 10.0 %collective-permute-start = (bf16[1024,128]{1,0:T(8,128)(2,1)}, bf16[1024,128]{1,0:T(8,128)(2,1)S(1)}, u32[]{:S(2)}, u32[]{:S(2)}) collective-permute-start(bf16[1024,128]{1,0:T(8,128)(2,1)} %get-tuple-element.591), channel_id=1, source_target_pairs={{480,0},{0,32},{32,64},{64,96},{96,128},{128,160},{160,192},{192,2... | collective-permute-start | bytes 786440 | tf_op jit(solution)/shard_map/while/body/eval_jaxpr/ppermute | solution.py:14
  212.4 10.0 %collective-permute-start = (bf16[1024,128]{1,0:T(8,128)(2,1)}, bf16[1024,128]{1,0:T(8,128)(2,1)S(1)}, u32[]{:S(2)}, u32[]{:S(2)}) collective-permute-start(bf16[1024,128]{1,0:T(8,128)(2,1)} %get-tuple-element.591), channel_id=1, source_target_pairs={{480,0},{0,32},{32,64},{64,96},{96,128},{128,160},{160,192},{192,2... | collective-permute-start | bytes 786440 | tf_op jit(solution)/shard_map/while/body/eval_jaxpr/ppermute | solution.py:14
  227.1 10.0 %collective-permute-start = (bf16[1024,128]{1,0:T(8,128)(2,1)}, bf16[1024,128]{1,0:T(8,128)(2,1)S(1)}, u32[]{:S(2)}, u32[]{:S(2)}) collective-permute-start(bf16[1024,128]{1,0:T(8,128)(2,1)} %get-tuple-element.591), channel_id=1, source_target_pairs={{480,0},{0,32},{32,64},{64,96},{96,128},{128,160},{160,192},{192,2... | collective-permute-start | bytes 786440 | tf_op jit(solution)/shard_map/while/body/eval_jaxpr/ppermute | solution.py:14
  241.9 10.0 %collective-permute-start = (bf16[1024,128]{1,0:T(8,128)(2,1)}, bf16[1024,128]{1,0:T(8,128)(2,1)S(1)}, u32[]{:S(2)}, u32[]{:S(2)}) collective-permute-start(bf16[1024,128]{1,0:T(8,128)(2,1)} %get-tuple-element.591), channel_id=1, source_target_pairs={{480,0},{0,32},{32,64},{64,96},{96,128},{128,160},{160,192},{192,2... | collective-permute-start | bytes 786440 | tf_op jit(solution)/shard_map/while/body/eval_jaxpr/ppermute | solution.py:14
  (79 other events, 237.6 us)
Sparse Core Ops, SparseCore 0:
  258.4 451.5 all-reduce.1
where the time goes:
time: 721 us; the launch traced here: 718 us
  waiting for transfers between devices  407 us (56%)
  blocking collectives  109 us (15%)
  matrix products  94.2 us (13%)
  starting transfers between devices  33.8 us (5%)
  local copies, waits for them, and re-layouts  31.4 us (4%)
  other arithmetic  25.3 us (4%)
  between operations  14.4 us (2%)
    psum x1, waiting for transfers between devices, per_device(): grad_residue, grad_rate = lax.psum((grad_part, rate_part), ('ctx', 'dp'))  339 us
    psum x1, blocking collectives, per_device(): grad_residue, grad_rate = lax.psum((grad_part, rate_part), ('ctx', 'dp'))  109 us
    ppermute x16, waiting for transfers between devices, from_behind(): return lax.ppermute(block, axis, route)  67.9 us
    ppermute x16, starting transfers between devices, from_behind(): return lax.ppermute(block, axis, route)  33.8 us
    dot_general x16, matrix products, pair_terms(): filt_spec = jnp.dot(residue, spectra[:modes], precision=HIGHEST)  30 us
    while x135, local copies, waits for them, and re-layouts  20.4 us
    dot_general x16, matrix products, split_dot(): jnp.dot(data, halves[1], preferred_element_type=jnp.float32)  19.2 us
    dot_general x16, matrix products, mode_spectra(): return jnp.dot(stacked, forward, precision=HIGHEST)  18 us
  transfers between devices with their start and end apart: 17, of which 16 were waited for; matrix products, arithmetic and copies ran while one was open for 9% of the time, Pallas kernels for 0%

commit v1 on v0

v1 whole, which is shorter than its diff:
```python
import functools
import math

import jax
import jax.numpy as jnp
from jax import lax
from jax.experimental import pallas as pl
from jax.experimental.pallas import tpu as pltpu
from jax.sharding import PartitionSpec as P

MESH = pl.DeviceIdType.MESH
F32 = jnp.float32
BF16 = jnp.bfloat16
TILE = 256
HALF = 8
LANES = 128


def filter_tables(rates, block, seq_len):
    modes = rates.shape[0]
    period = 2 * modes + 2
    number = jnp.arange(modes, dtype=jnp.int32)[:, None] + 1

    def angle(steps):
        return (number * steps[None, :] % period).astype(F32) * (2.0 * math.pi / period)

    def decay(steps):
        return jnp.exp(-rates[:, None] * steps.astype(F32)[None, :] / seq_len)

    pos = jnp.arange(block, dtype=jnp.int32)
    rise = jnp.exp(rates[:, None] * pos.astype(F32)[None, :] / seq_len)
    cos_p, sin_p = jnp.cos(angle(pos)), jnp.sin(angle(pos))
    wrap = pos + seq_len
    near, far = decay(pos), decay(wrap)
    near_c, near_s = near * cos_p, near * sin_p
    far_c, far_s = far * jnp.cos(angle(wrap)), far * jnp.sin(angle(wrap))
    src_c, src_s = rise * cos_p, rise * sin_p
    causal = pos[:, None] >= pos[None, :]
    out_c = jnp.where(causal[None], near_c[:, :, None], far_c[:, :, None])
    out_s = jnp.where(causal[None], near_s[:, :, None], far_s[:, :, None])
    power = out_c * src_c[:, None, :] + out_s * src_s[:, None, :]
    gap = pos[:, None] - pos[None, :]
    delay = jnp.where(causal, gap, gap + seq_len).astype(F32) / seq_len
    slope = -power * delay[None]
    dense = jnp.stack([power, slope], axis=1).reshape(2 * modes * block, block).astype(BF16)

    def state(steps):
        real = decay(steps) * jnp.cos(angle(steps))
        imag = decay(steps) * jnp.sin(angle(steps))
        weight = (steps.astype(F32) / seq_len)[None, :]
        rows = jnp.stack([real, imag, real * weight, imag * weight], axis=0)
        rows = rows.reshape(4, modes // HALF, HALF, block).transpose(1, 0, 2, 3)
        return rows.reshape(4 * modes, block).astype(BF16), real, imag

    into, _, _ = state(block - 1 - pos)
    onto, real, imag = state(pos + 1)
    spread = jnp.stack([real, -imag], axis=0).reshape(2, modes // HALF, HALF, block)
    spread = spread.transpose(3, 1, 0, 2).reshape(block, 2 * modes).astype(BF16)
    return dense, into, onto, spread


def local_kernel(ids_ref, table_ref, short_ref, dense_ref, into_ref, onto_ref, res_ref, skip_ref,
                 gout_ref, query_ref, base_ref, msg_ref, feat, sums):
    rows = ids_ref.shape[0]
    block = dense_ref.shape[1]
    modes = res_ref.shape[0]
    vocab = table_ref.shape[2]
    columns = lax.broadcasted_iota(jnp.int32, (rows, vocab), 1)
    onehot = jnp.where(columns == ids_ref[...], 1.0, 0.0).astype(BF16)
    mixed = []
    for part in range(3):
        feat[part] = lax.dot_general(
            onehot, table_ref[part], (((1,), (1,)), ((), ())), preferred_element_type=F32
        )
        total = short_ref[part, 0:1, :] * feat[part, 2 : 2 + block, :]
        for tap in range(1, 7):
            total = total + short_ref[part, tap : tap + 1, :] * feat[part, 2 + tap : 2 + tap + block, :]
        mixed.append(total)
    query = mixed[0]
    gated = (mixed[1] * mixed[2]).astype(BF16)
    query_ref[...] = query
    dconv = query * gout_ref[...].astype(F32).T
    base = skip_ref[...] * gated.astype(F32)
    for mode in range(modes):
        for kind in range(2):
            row = (2 * mode + kind) * block
            term = jnp.dot(dense_ref[row : row + block, :], gated, preferred_element_type=F32)
            if kind == 0:
                base = base + res_ref[mode : mode + 1, :] * term
            slot = (mode // HALF) * 2 * HALF + kind * HALF + mode % HALF
            sums[slot : slot + 1, :] = jnp.sum(dconv * term, axis=0, keepdims=True)
    base_ref[...] = base
    upper = jnp.dot(into_ref[...], gated, preferred_element_type=F32).astype(BF16)
    lower = jnp.dot(onto_ref[...], dconv.astype(BF16), preferred_element_type=F32).astype(BF16)
    totals = sums[...].astype(BF16)
    for group in range(TILE // LANES):
        lane = slice(group * LANES, (group + 1) * LANES)
        for half in range(2):
            slot = group * 2 + half
            msg_ref[slot, 0:32, :] = upper[half * 32 : half * 32 + 32, lane]
            msg_ref[slot, 32:64, :] = lower[half * 32 : half * 32 + 32, lane]
            msg_ref[slot, 64:80, :] = totals[half * 16 : half * 16 + 16, lane]


def exchange_kernel(ctx_n, dp_n, rows_n, msg_ref, turn_ref, res_ref, state_ref, grad_ref,
                    got, backs, terms, parts, column, sem_a, sem_b, sem_c, sem_d, sem_e,
                    rsem_a, rsem_b, rsem_c, rsem_d, rsem_e, local_sem):
    me = lax.axis_index("ctx")
    rank = lax.axis_index("dp")
    low = lax.rem(rank, rows_n)
    base = rank - low

    barrier = pltpu.get_barrier_semaphore()

    def greet_ctx(step, carry):
        pl.semaphore_signal(barrier, inc=1, device_id={"ctx": lax.rem(me + step, ctx_n)}, device_id_type=MESH)
        return carry

    def greet_dp(step, carry):
        pl.semaphore_signal(barrier, inc=1, device_id={"dp": lax.rem(rank + step, dp_n)}, device_id_type=MESH)
        return carry

    lax.fori_loop(1, ctx_n, greet_ctx, 0)
    lax.fori_loop(1, dp_n, greet_dp, 0)
    pl.semaphore_wait(barrier, ctx_n - 1 + dp_n - 1)

    def run(count, make):
        def body(step, carry):
            make(step).start()
            return carry
        lax.fori_loop(1, count, body, 0)

    def land(count, make):
        def body(step, carry):
            make(step).wait_recv()
            return carry
        lax.fori_loop(1, count, body, 0)

    def left(count, make):
        def body(step, carry):
            make(step).wait_send()
            return carry
        lax.fori_loop(1, count, body, 0)

    def over_ctx(source, target, send, recv):
        def make(step, arriving):
            peer = lax.rem(me + step, ctx_n)
            slot = lax.rem(me + ctx_n - step, ctx_n) if arriving else me
            return pltpu.make_async_remote_copy(
                src_ref=source(peer), dst_ref=target.at[slot], send_sem=send.at[step],
                recv_sem=recv.at[slot], device_id={"ctx": peer}, device_id_type=MESH)
        return (lambda step: make(step, False)), (lambda step: make(step, True))

    out_a, in_a = over_ctx(lambda peer: msg_ref.at[peer], got, sem_a, rsem_a)
    run(ctx_n, out_a)
    own = pltpu.make_async_copy(msg_ref.at[me], got.at[me], local_sem.at[0])
    own.start()
    own.wait()
    land(ctx_n, in_a)

    turn_c, turn_s, last_c, last_s = (turn_ref[i] for i in range(4))

    def states(index, first):
        pair = got[index, first : first + 16, :].astype(F32)
        return pair[:HALF], pair[HALF:]

    step_len = 1.0 / ctx_n

    def times_turn(real, imag):
        return real * turn_c - imag * turn_s, real * turn_s + imag * turn_c

    def times_last(real, imag):
        return real * last_c - imag * last_s, real * last_s + imag * last_c

    zero = jnp.zeros((HALF, LANES), F32)

    def advance(carry, index):
        hr, hi, dr, di = carry
        ur, ui = states(index, 0)
        wr, wi = states(index, 16)
        nr, ni = times_turn(hr, hi)
        er, ei = times_turn(dr + step_len * hr, di + step_len * hi)
        return nr + ur, ni + ui, er + wr, ei + wi

    def warm(index, carry):
        return advance(carry, index)

    start = lax.fori_loop(1, ctx_n, warm, (zero, zero, zero, zero))
    span = step_len * (ctx_n - 2)

    def visit(index, carry):
        hr, hi, dr, di, gsum, dsum = carry
        backs[index, 0:16, :] = jnp.concatenate([hr, hi], axis=0).astype(BF16)
        vr, vi = states(index, 32)
        xr, xi = states(index, 48)
        g0, d0 = states(index, 64)
        gsum = gsum + (g0 + (vr * hr - vi * hi))
        dsum = dsum + (d0 - ((xr * hr - xi * hi) + (vr * dr - vi * di)))
        old = lax.rem(index + 1, ctx_n)
        ur, ui = states(old, 0)
        wr, wi = states(old, 16)
        lr, li = times_last(ur, ui)
        pr, pi_ = times_last(wr + span * ur, wi + span * ui)
        hr, hi, dr, di = advance((hr - lr, hi - li, dr - pr, di - pi_), index)
        return hr, hi, dr, di, gsum, dsum

    final = lax.fori_loop(0, ctx_n, visit, start + (zero, zero))
    gsum = final[4]
    dsum = final[5] * res_ref[...]

    out_b, in_b = over_ctx(lambda peer: backs.at[peer], state_ref, sem_b, rsem_b)
    for row in range(HALF):
        terms[row] = gsum[row : row + 1, :]
        terms[HALF + row] = dsum[row : row + 1, :]

    def over_dp(arriving):
        def make(step):
            peer = lax.rem(rank + step, dp_n)
            slot = lax.rem(rank + dp_n - step, dp_n) if arriving else rank
            return pltpu.make_async_remote_copy(
                src_ref=terms.at[lax.rem(peer, rows_n)], dst_ref=parts.at[slot], send_sem=sem_c.at[step],
                recv_sem=rsem_c.at[slot], device_id={"dp": peer}, device_id_type=MESH)
        return make

    run(dp_n, over_dp(False))
    keep = pltpu.make_async_copy(terms.at[low], parts.at[rank], local_sem.at[1])
    keep.start()
    run(ctx_n, out_b)
    mine = pltpu.make_async_copy(backs.at[me], state_ref.at[me], local_sem.at[2])
    mine.start()
    keep.wait()
    land(dp_n, over_dp(True))
    column[...] = jnp.sum(parts[...], axis=0)

    def over_rows(arriving):
        def make(step):
            other = lax.rem(low + step, rows_n)
            slot = lax.rem(low + rows_n - step, rows_n) if arriving else low
            return pltpu.make_async_remote_copy(
                src_ref=column, dst_ref=grad_ref.at[me, slot], send_sem=sem_d.at[step],
                recv_sem=rsem_d.at[slot], device_id={"dp": base + other}, device_id_type=MESH)
        return make

    run(rows_n, over_rows(False))
    place = pltpu.make_async_copy(column, grad_ref.at[me, low], local_sem.at[3])
    place.start()
    place.wait()
    land(rows_n, over_rows(True))
    out_e, in_e = over_ctx(lambda peer: grad_ref.at[me], grad_ref, sem_e, rsem_e)
    run(ctx_n, out_e)
    mine.wait()
    land(ctx_n, in_b)
    land(ctx_n, in_e)
    left(ctx_n, out_a)
    left(ctx_n, out_b)
    left(dp_n, over_dp(False))
    left(rows_n, over_rows(False))
    left(ctx_n, out_e)


def finish_kernel(state_ref, res_ref, spread_ref, query_ref, base_ref, out_ref):
    columns = []
    for group in range(TILE // LANES):
        columns.append(jnp.concatenate(
            [state_ref[group * 2].astype(F32), state_ref[group * 2 + 1].astype(F32)], axis=0))
    state = (jnp.concatenate(columns, axis=1) * res_ref[...]).astype(BF16)
    conv = jnp.dot(spread_ref[...], state, preferred_element_type=F32)
    out_ref[...] = (query_ref[...] * (base_ref[...] + conv)).T.astype(BF16)


def per_device(dp_n, token_ids, feature_table, short_weight, residue, rates, skip_gain, grad_out):
    block = token_ids.shape[1]
    ctx_n = lax.axis_size("ctx")
    seq_len = block * ctx_n
    channels, modes = residue.shape
    vocab = feature_table.shape[1]
    taps = short_weight.shape[1]
    rows_n = 2 * HALF
    me = lax.axis_index("ctx")

    ids = token_ids[0]
    route = [((i - 1) % ctx_n, i) for i in range(ctx_n)]
    previous = lax.ppermute(ids[block - (taps - 1) :], "ctx", route)
    ids_col = jnp.concatenate([jnp.full((2,), -1, jnp.int32), previous, ids])[:, None]
    rows = ids_col.shape[0]

    dense, into, onto, spread = filter_tables(rates, block, seq_len)
    short = jnp.pad(short_weight.T, ((0, 1), (0, 0))).reshape(8, 3, channels).transpose(1, 0, 2)
    table = feature_table.reshape(3, channels, vocab)
    res_t = residue.T
    whole = lambda shape: pl.BlockSpec(shape, lambda i: (0,) * len(shape))
    lanes = lambda n: pl.BlockSpec((n, TILE), lambda i: (0, i))

    query, base, msg = pl.pallas_call(
        local_kernel,
        grid=(channels // TILE,),
        in_specs=[
            whole((rows, 1)),
            pl.BlockSpec((3, TILE, vocab), lambda i: (0, i, 0)),
            pl.BlockSpec((3, 8, TILE), lambda i: (0, 0, i)),
            whole(dense.shape), whole(into.shape), whole(onto.shape),
            lanes(modes), lanes(1),
            pl.BlockSpec((TILE, block), lambda i: (i, 0)),
        ],
        out_specs=[lanes(block), lanes(block),
                   pl.BlockSpec((2 * TILE // LANES, 80, LANES), lambda i: (i, 0, 0))],
        out_shape=[jax.ShapeDtypeStruct((block, channels), F32),
                   jax.ShapeDtypeStruct((block, channels), F32),
                   jax.ShapeDtypeStruct((ctx_n, 80, LANES), BF16)],
        scratch_shapes=[pltpu.VMEM((3, rows, TILE), F32), pltpu.VMEM((2 * modes, TILE), F32)],
        compiler_params=pltpu.CompilerParams(vmem_limit_bytes=40 * 1024 * 1024),
    )(ids_col, table, short, dense, into, onto, res_t, skip_gain[None, :], grad_out[0])

    half, group = me % 2, me // 2
    own_rates = lax.dynamic_slice(rates, (half * HALF,), (HALF,))
    own_mode = half * HALF + 1 + jnp.arange(HALF, dtype=jnp.int32)
    period = 2 * modes + 2

    def turn(steps):
        angle = (own_mode * steps % period).astype(F32) * (2.0 * math.pi / period)
        size = jnp.exp(-own_rates * (steps / seq_len))
        return [size * jnp.cos(angle), size * jnp.sin(angle)]

    turns = jnp.stack(turn(block) + turn(block * (ctx_n - 2)))
    turns = jnp.broadcast_to(turns[:, :, None], (4, HALF, LANES))
    own_res = lax.dynamic_slice(res_t, (half * HALF, group * LANES), (HALF, LANES))

    dma = pltpu.SemaphoreType.DMA
    vmem = pl.BlockSpec(memory_space=pltpu.VMEM)
    states, grads = pl.pallas_call(
        functools.partial(exchange_kernel, ctx_n, dp_n, rows_n),
        in_specs=[vmem] * 3,
        out_specs=[vmem] * 2,
        out_shape=[jax.ShapeDtypeStruct((ctx_n, 16, LANES), BF16),
                   jax.ShapeDtypeStruct((ctx_n, rows_n, 1, LANES), F32)],
        scratch_shapes=[
            pltpu.VMEM((ctx_n, 80, LANES), BF16),
            pltpu.VMEM((ctx_n, 16, LANES), BF16),
            pltpu.VMEM((rows_n, 1, LANES), F32),
            pltpu.VMEM((dp_n, 1, LANES), F32),
            pltpu.VMEM((1, LANES), F32),
            dma((ctx_n,)), dma((ctx_n,)), dma((dp_n,)), dma((rows_n,)), dma((ctx_n,)),
            dma((ctx_n,)), dma((ctx_n,)), dma((dp_n,)), dma((rows_n,)), dma((ctx_n,)),
            dma((4,)),
        ],
        compiler_params=pltpu.CompilerParams(collective_id=0, has_side_effects=True),
    )(msg, turns, own_res)

    res_rows = jnp.concatenate([res_t[:HALF], res_t[:HALF], res_t[HALF:], res_t[HALF:]], axis=0)
    mixed = pl.pallas_call(
        finish_kernel,
        grid=(channels // TILE,),
        in_specs=[
            pl.BlockSpec((2 * TILE // LANES, 16, LANES), lambda i: (i, 0, 0)),
            lanes(2 * modes), whole((block, 2 * modes)), lanes(block), lanes(block),
        ],
        out_specs=pl.BlockSpec((TILE, block), lambda i: (i, 0)),
        out_shape=jax.ShapeDtypeStruct((channels, block), BF16),
    )(states, res_rows, spread, query, base)

    parts = grads.reshape(ctx_n // 2, 2, 2, HALF, LANES)
    grad_residue = parts[:, :, 0].transpose(0, 3, 1, 2).reshape(channels, modes)
    grad_rate = jnp.sum(parts[:, :, 1], axis=(0, 3)).reshape(modes)
    return (mixed[None], grad_residue, grad_rate)


def solution(mesh):
    return jax.shard_map(
        functools.partial(per_device, mesh.shape["dp"]),
        mesh=mesh,
        in_specs=(P("dp", "ctx"), P(), P(), P(), P(), P(), P("dp", None, "ctx")),
        out_specs=(P("dp", None, "ctx"), P(), P()),
        check_vma=False,
    )
```

time: 721 us -> 80.8 us (0.11)
  waiting for transfers between devices: 407 us -> 0.01 us
  blocking collectives: 109 us -> 0 us
  matrix products: 94.2 us -> 0 us
  Pallas kernels: 0 us -> 59.3 us
  starting transfers between devices: 33.8 us -> 4.57 us
  local copies, waits for them, and re-layouts: 31.4 us -> 9.9 us
  other arithmetic: 25.3 us -> 5.62 us
  between operations: 14.4 us -> 0.95 us
    psum x1 -> x0, waiting for transfers between devices: 339 us -> none  [per_device(): grad_residue, grad_rate = lax.psum((grad_part, rate_part), ('ctx', 'dp'))]
    psum x1 -> x0, blocking collectives: 109 us -> none  [per_device(): grad_residue, grad_rate = lax.psum((grad_part, rate_part), ('ctx', 'dp'))]
    dot_general x84 -> x0, matrix products: 94.2 us -> none  [the longest x16 30 us: pair_terms(): filt_spec = jnp.dot(residue, spectra[:modes], precision=HIGHEST)]
    ppermute x16 -> x1, waiting for transfers between devices: 67.9 us -> 0.01 us  [per_device(): previous = lax.ppermute(ids[block - (taps - 1):], 'ctx', route)]
    pallas_call x0 -> x3, Pallas kernels: none -> 59.3 us  [the longest x1 46.5 us: per_device(): pl.pallas_call(functools.partial(exchange_kernel, ctx_n, dp_n, rows_n), i...]
    ppermute x16 -> x1, starting transfers between devices: 33.8 us -> 4.57 us  [per_device(): previous = lax.ppermute(ids[block - (taps - 1):], 'ctx', route)]
    while x135 -> x0, local copies, waits for them, and re-layouts: 20.4 us -> none
    select_n x33 -> x0, other arithmetic: 10 us -> none  [the longest x16 9.3 us: packed_product(): jnp.where(leading, left_re * right_re, left_re * right_re + left_im * rig...]
  transfers between devices with their start and end apart: 17 -> 1, of which waited for: 16 -> 0; matrix products, arithmetic and copies ran while one was open for 9% -> 9% of each run, Pallas kernels for 0% -> 0%
where the time goes in v1:
time: 80.8 us; the launch traced here: 80.4 us
  Pallas kernels  59.3 us (73%)
  local copies, waits for them, and re-layouts  9.9 us (12%)
  other arithmetic  5.62 us (7%)
  starting transfers between devices  4.57 us (6%)
  between operations  0.95 us (1%)
    pallas_call x1, Pallas kernels, per_device(): pl.pallas_call(functools.partial(exchange_kernel, ctx_n, dp_n, rows_n), i...  46.5 us
    pallas_call x1, Pallas kernels, per_device(): pl.pallas_call(local_kernel, grid=(channels // TILE,), in_specs=[whole((r...  9.08 us
    ppermute x1, starting transfers between devices, per_device(): previous = lax.ppermute(ids[block - (taps - 1):], 'ctx', route)  4.57 us
    unnamed x18, local copies, waits for them, and re-layouts  4.23 us
    pallas_call x1, Pallas kernels, per_device(): pl.pallas_call(finish_kernel, grid=(channels // TILE,), in_specs=[pl.Bloc...  3.76 us
  transfers between devices with their start and end apart: 1, of which 0 were waited for; matrix products, arithmetic and copies ran while one was open for 9% of the time, Pallas kernels for 0%

profile of v1, /device:TPU:1, one launch (start us, length us, event | category | flops | bytes accessed | tf_op | source)
XLA Modules:
  0.0 80.4 jit_solution(12057261762816652065)
XLA Ops:
  0.7 0.8 slice_bitcast_fusion.1
  1.5 4.6 %collective-permute-start = (s32[6]{0:T(128)S(1)}, s32[6]{0:T(128)S(1)}, u32[]{:S(2)}, u32[]{:S(2)}) collective-permute-start(s32[6]{0:T(128)S(1)} %slice_bitcast_fusion.1), channel_id=1, source_target_pairs={{480,0},{0,32},{32,64},{64,96},{96,128},{128,160},{160,192},{192,2... | collective-permute-start | bytes 80 | tf_op jit(solution)/shard_map/ppermute | solution.py:283
  6.2 0.7 neg.34
  7.0 0.7 multiply_bitcast_fusion.3
  7.8 0.2 multiply_convert_fusion.2
  8.0 0.7 copy.14.spread_ref
  8.7 1.3 %dynamic-slice_bitcast_fusion.res_ref = f32[8,128]{1,0:T(8,128)} fusion(f32[1024,16]{0,1:T(8,128)} %param.10, s32[]{:T(128)S(6)} %select_n.188, s32[]{:T(128)S(6)} %select_n.184), kind=kLoop, calls=%fused_computation.69 | loop fusion | bytes 8200 | tf_op jit(solution)/shard_map/dynamic_slice | solution.py:326
  10.0 0.8 fusion.40
  10.8 0.8 %fusion.23 = (f32[16,128]{1,0:T(8,128)S(1)}, f32[16,128]{1,0:T(8,128)S(1)}, f32[16,128]{1,0:T(8,128)S(1)}, f32[16,128]{1,0:T(8,128)S(1)}, f32[16,128]{1,0:T(8,128)S(1)}, /*index=5*/f32[16,128]{1,0:T(8,128)S(1)}) fusion(s32[16]{0:T(128)S(1)} %iota_add_fusion.3, f32[128]{0:T(128)S(1)} %get-tuple-element.48, f32[16]{0:T(128)S(1)} %neg.34, f32[16]{0:T(128)} %param.11, ...), kind=kLoop, calls=%fused_computation.58 | loop fusion | flops 61440 | bytes 50880 | tf_op jit(solution)/shard_map/mul | solution.py:35
  11.6 1.3 %fusion = (bf16[16,1,128,128]{3,2,1,0:T(8,128)(2,1)S(1)}, bf16[16,1,128,128]{3,2,1,0:T(8,128)(2,1)S(1)}) fusion(f32[16,128]{1,0:T(8,128)S(1)} %get-tuple-element.40, f32[16,128]{1,0:T(8,128)S(1)} %get-tuple-element.42, f32[16,128]{1,0:T(8,128)S(1)} %get-tuple-element.37, f32[16,128]{1,0:T(8,128)S(1)} %get-tuple-element.41, ...), kind=kLoop, calls=%fused_computation.3 | loop fusion | flops 2359296 | bytes 1179648 | tf_op jit(solution)/shard_map/convert.10
  12.8 0.1 pad_maximum_fusion
  13.0 0.7 pad_maximum_fusion.1.res_ref
  13.8 0.1 copy.13.ids_ref
  13.9 1.9 %copy-done = bf16[3072,512]{1,0:T(8,128)(2,1)S(1)} copy-done((bf16[3072,512]{1,0:T(8,128)(2,1)S(1)}, bf16[3072,512]{1,0:T(8,128)(2,1)}, u32[]{:S(2)}) %copy-start) | copy-done | bytes 3145752
  15.8 9.1 %shard_map.94 = (f32[128,1024]{1,0:T(8,128)S(1)}, f32[128,1024]{1,0:T(8,128)S(1)}, bf16[16,80,128]{2,1,0:T(8,128)(2,1)S(1)}) custom-call(s32[136,1]{1,0:T(8,128)S(1)} %copy.13.ids_ref, bf16[3,1024,512]{2,1,0:T(8,128)(2,1)S(1)} %bitcast.42, f32[3,8,1024]{2,1,0:T(8,128)S(1)} %bitcast.46, bf16[4096,128]{1,0:T(8,128)(2,1)S(1)} %bitcast.41, ...), custom_call_target="tpu_custom_call" | custom-call | tf_op jit(solution)/shard_map/pallas_call | solution.py:294
  24.9 0.8 copy-done.2
  25.7 0.8 copy-done.3
  26.5 0.7 copy-done.4
  27.2 0.7 broadcast_in_dim.54.turn_ref
  27.9 46.5 %shard_map.95 = (bf16[16,16,128]{2,1,0:T(8,128)(2,1)}, f32[16,16,1,128]{3,2,1,0:T(1,128)}) custom-call(bf16[16,80,128]{2,1,0:T(8,128)(2,1)} %copy-done.4, f32[4,8,128]{2,1,0:T(8,128)} %broadcast_in_dim.54.turn_ref, f32[8,128]{1,0:T(8,128)} %dynamic-slice_bitcast_fusion.res_ref), custom_call_target="tpu_custom_call" | custom-call | tf_op jit(solution)/shard_map/pallas_call | solution.py:330
  74.4 1.0 %slice_reduce_fusion = (f32[2,8]{1,0:T(2,128)S(1)}, f32[8,128,2,8]{1,3,2,0:T(8,128)S(1)}) fusion(f32[8,2,2,8,128]{4,3,2,1,0:T(8,128)} %bitcast.52), kind=kLoop, calls=%fused_computation.8 | loop fusion | flops 16368 | bytes 196672 | tf_op jit(solution)/shard_map/reduce_sum | solution.py:363
  75.4 0.6 copy.17
  76.0 0.6 reshape.942
  76.6 3.8 %shard_map.96 = bf16[1024,128]{1,0:T(8,128)(2,1)} custom-call(bf16[16,16,128]{2,1,0:T(8,128)(2,1)} %get-tuple-element.9.state_ref, f32[32,1024]{1,0:T(8,128)} %pad_maximum_fusion.1.res_ref, bf16[128,32]{1,0:T(8,128)(2,1)} %copy.14.spread_ref, f32[128,1024]{1,0:T(8,128)} %copy-done.2, f32[128,1024]{1,0:T(8,128)} %copy-done.3), custom_call_target="tpu_custom_call" | custom-call | tf_op jit(solution)/shard_map/pallas_call | solution.py:350
  (35 shorter events, 0.4 us)
Async XLA Ops:
  0.6 13.1 %copy-start.8 = (s32[1,128]{1,0:T(1,128)S(1)}, s32[1,128]{1,0:T(1,128)}, u32[]{:S(2)}) copy-start(s32[1,128]{1,0:T(1,128)} %param.7) | copy-start | bytes 1540
  0.6 12.3 %copy-start.1 = (f32[1024,16]{0,1:T(8,128)S(1)}, f32[1024,16]{0,1:T(8,128)}, u32[]{:S(2)}) copy-start(f32[1024,16]{0,1:T(8,128)} %param.10) | copy-start | bytes 196612
  0.7 12.3 %copy-start.7 = (f32[3072,7]{0,1:T(8,128)S(1)}, f32[3072,7]{0,1:T(8,128)}, u32[]{:S(2)}) copy-start(f32[3072,7]{0,1:T(8,128)} %param.9) | copy-start | bytes 258052
  0.7 13.2 %copy-start.6 = (f32[1024]{0:T(1024)S(1)}, f32[1024]{0:T(1024)}, u32[]{:S(2)}) copy-start(f32[1024]{0:T(1024)} %param.12) | copy-start | bytes 12292
  0.7 13.2 %copy-start.5 = (bf16[1,1024,128]{2,1,0:T(8,128)(2,1)S(1)}, bf16[1,1024,128]{2,1,0:T(8,128)(2,1)}, u32[]{:S(2)}) copy-start(bf16[1,1024,128]{2,1,0:T(8,128)(2,1)} %param.13) | copy-start | bytes 786436
  1.5 12.2 %collective-permute-start = (s32[6]{0:T(128)S(1)}, s32[6]{0:T(128)S(1)}, u32[]{:S(2)}, u32[]{:S(2)}) collective-permute-start(s32[6]{0:T(128)S(1)} %slice_bitcast_fusion.1), channel_id=1, source_target_pairs={{480,0},{0,32},{32,64},{64,96},{96,128},{128,160},{160,192},{192,2... | collective-permute-start | bytes 80 | tf_op jit(solution)/shard_map/ppermute | solution.py:283
  13.9 1.9 %copy-start = (bf16[3072,512]{1,0:T(8,128)(2,1)S(1)}, bf16[3072,512]{1,0:T(8,128)(2,1)}, u32[]{:S(2)}) copy-start(bf16[3072,512]{1,0:T(8,128)(2,1)} %param.8) | copy-start | bytes 9437188
  24.9 0.8 %copy-start.2 = (f32[128,1024]{1,0:T(8,128)}, f32[128,1024]{1,0:T(8,128)S(1)}, u32[]{:S(2)}) copy-start(f32[128,1024]{1,0:T(8,128)S(1)} %get-tuple-element.10.query_ref) | copy-start | bytes 1572868
  25.7 0.8 copy-start.3
  26.5 0.7 copy-start.4

commit v2 on v0

v2 whole, which is shorter than its diff:
```python
import functools
import math

import jax
import jax.numpy as jnp
from jax import lax
from jax.experimental import pallas as pl
from jax.experimental.pallas import tpu as pltpu
from jax.sharding import PartitionSpec as P

MESH = pl.DeviceIdType.MESH
F32 = jnp.float32
BF16 = jnp.bfloat16
TILE = 256
HALF = 8
LANES = 128


def ids_kernel(ctx_n, ids_ref, prev_ref, send_sem, recv_sem):
    me = lax.axis_index("ctx")
    right, left = lax.rem(me + 1, ctx_n), lax.rem(me + ctx_n - 1, ctx_n)
    barrier = pltpu.get_barrier_semaphore()
    pl.semaphore_signal(barrier, inc=1, device_id={"ctx": left}, device_id_type=MESH)
    pl.semaphore_wait(barrier, 1)
    copy = pltpu.make_async_remote_copy(
        src_ref=ids_ref, dst_ref=prev_ref, send_sem=send_sem, recv_sem=recv_sem,
        device_id={"ctx": right}, device_id_type=MESH)
    copy.start()
    copy.wait()


def layer_kernel(ctx_n, dp_n, rates_ref, ids_hbm, prev_hbm, short_hbm, res_hbm, skip_hbm, table_hbm, gout_hbm,
                 out_hbm, gres_ref, grate_ref,
                 ids_ref, prev_ref, short_ref, res_ref, skip_ref, out_ref, gated_s, dconv_s, late, got_late,
                 table, gout, dense, into, onto, spread, rate_rows, feat, sums, query_s, base_s,
                 msg, got, backs, state, parts, grads,
                 sem_a, sem_b, sem_c, sem_e, sem_f, rsem_a, rsem_b, rsem_c, rsem_e, rsem_f, local_sem):
    me = lax.axis_index("ctx")
    rank = lax.axis_index("dp")
    modes, channels = res_ref.shape
    block = out_ref.shape[1]
    vocab = table.shape[2]
    taps = short_ref.shape[0]
    seq_len = block * ctx_n
    tiles = channels // TILE
    period = 2 * modes + 2

    barrier = pltpu.get_barrier_semaphore()

    def greet_dp(step, carry):
        pl.semaphore_signal(barrier, inc=1, device_id={"dp": lax.rem(rank + step, dp_n)}, device_id_type=MESH)
        return carry

    def greet_ctx(step, carry):
        pl.semaphore_signal(barrier, inc=1, device_id={"ctx": lax.rem(me + step, ctx_n)}, device_id_type=MESH)
        return carry

    lax.fori_loop(1, dp_n, greet_dp, 0)
    lax.fori_loop(1, ctx_n, greet_ctx, 0)

    small = []
    pairs = ((ids_hbm, ids_ref), (prev_hbm, prev_ref), (short_hbm, short_ref), (res_hbm, res_ref),
             (skip_hbm, skip_ref), (gout_hbm, gout))
    for index, (source, target) in enumerate(pairs):
        small.append(pltpu.make_async_copy(source, target, local_sem.at[tiles + index]))
        small[-1].start()
    loads = []
    for tile in range(tiles):
        part = pl.ds(tile * TILE, TILE)
        loads.append(pltpu.make_async_copy(table_hbm.at[:, part], table.at[:, part], local_sem.at[tile]))
        loads[-1].start()

    def wave_angle(product):
        turns = jnp.floor(product * (1.0 / period))
        return (product - period * turns) * (2.0 * math.pi / period)

    for mode in range(modes):
        rate_rows[mode : mode + 1, :] = jnp.full((1, LANES), rates_ref[mode], F32)
    decay_rows = rate_rows[...] * (-1.0 / seq_len)
    number = lax.broadcasted_iota(jnp.int32, (modes, block), 0).astype(F32) + 1.0
    lane = lax.broadcasted_iota(jnp.int32, (modes, block), 1).astype(F32)

    def fill(ref, steps):
        size = jnp.exp(decay_rows * steps)
        angle = wave_angle(number * steps)
        real, imag = size * jnp.cos(angle), size * jnp.sin(angle)
        weight = steps * (1.0 / seq_len)
        for index, value in enumerate((real, imag, real * weight, imag * weight)):
            for half in range(2):
                ref[half * 32 + index * HALF : half * 32 + (index + 1) * HALF, :] = value[half * HALF : (half + 1) * HALF]
        return real, imag

    fill(into, (block - 1.0) - lane)
    real, imag = fill(onto, lane + 1.0)
    spread[...] = jnp.concatenate(
        [real[:HALF], -imag[:HALF], real[HALF:], -imag[HALF:], jnp.zeros((block - 2 * modes, block), F32)],
        axis=0).T.astype(BF16)

    gap = (lax.broadcasted_iota(jnp.int32, (block, block), 0)
           - lax.broadcasted_iota(jnp.int32, (block, block), 1)).astype(F32)
    delay = jnp.where(gap < 0.0, gap + seq_len, gap)
    base_wave = jnp.cos(wave_angle(delay))
    share = delay * (-1.0 / seq_len)

    def fill_dense(mode, carry):
        before, now = carry
        power = jnp.exp(share * rates_ref[mode]) * now
        row = pl.multiple_of(mode * 2 * block, 2 * block)
        dense[pl.ds(row, block), :] = power.astype(BF16)
        dense[pl.ds(row + block, block), :] = (power * share).astype(BF16)
        return now, 2.0 * base_wave * now - before


    for copy in small:
        copy.wait()

    def spell(ref):
        square = jnp.broadcast_to(ref[...].astype(F32), (block, block)).T
        return jnp.concatenate([square] * (vocab // block), axis=1)

    symbols = jnp.concatenate([spell(prev_ref)[block - 8 :], spell(ids_ref)], axis=0)
    columns = lax.broadcasted_iota(jnp.int32, symbols.shape, 1).astype(F32)
    onehot = jnp.where(columns == symbols, 1.0, 0.0).astype(BF16)

    def halves(value):
        upper = value.astype(BF16)
        return upper, (value - upper.astype(F32)).astype(BF16)

    into_b = jnp.concatenate(halves(into[...]), axis=0)
    onto_b = jnp.concatenate(halves(onto[...]), axis=0)
    states_n = 4 * modes

    for tile in range(tiles):
        loads[tile].wait()
        at = tile * TILE
        cols = pl.ds(at, TILE)
        mixed = []
        for part in range(3):
            feat[part] = lax.dot_general(
                onehot, table[part, cols, :], (((1,), (1,)), ((), ())), preferred_element_type=F32)
            wide = pl.ds(part * channels + at, TILE)
            total = short_ref[0:1, wide] * feat[part, 2 : 2 + block, :]
            for tap in range(1, taps):
                total = total + short_ref[tap : tap + 1, wide] * feat[part, 2 + tap : 2 + tap + block, :]
            mixed.append(total)
        gated = (mixed[1] * mixed[2]).astype(BF16)
        dconv = mixed[0] * gout[cols, :].astype(F32).T
        query_s[:, cols] = mixed[0]
        gated_s[:, cols] = gated
        dconv_s[:, cols] = dconv
        upper = jnp.dot(into_b, gated, preferred_element_type=F32)
        upper = upper[:states_n] + upper[states_n:]
        dconv_u, dconv_l = halves(dconv)
        lower = jnp.dot(onto_b, dconv_u, preferred_element_type=F32)
        lower = lower[:states_n] + lower[states_n:]
        lower = lower + jnp.dot(onto_b[:states_n], dconv_l, preferred_element_type=F32)
        for group in range(TILE // LANES):
            cut = slice(group * LANES, (group + 1) * LANES)
            for half in range(2):
                slot = (TILE // LANES * tile + group) * 2 + half
                msg[slot, 0:32, :] = upper[half * 32 : half * 32 + 32, cut]
                msg[slot, 32:64, :] = lower[half * 32 : half * 32 + 32, cut]

    lax.fori_loop(0, modes, fill_dense, (jnp.ones((block, block), F32), base_wave))
    pl.semaphore_wait(barrier, ctx_n - 1 + dp_n - 1)

    def run(count, make):
        def body(step, carry):
            make(step).start()
            return carry
        lax.fori_loop(1, count, body, 0)

    def land(count, make):
        def body(step, carry):
            make(step).wait_recv()
            return carry
        lax.fori_loop(1, count, body, 0)

    def left(count, make):
        def body(step, carry):
            make(step).wait_send()
            return carry
        lax.fori_loop(1, count, body, 0)

    def over_ctx(source, target, send, recv):
        def make(step, arriving):
            peer = lax.rem(me + step, ctx_n)
            slot = lax.rem(me + ctx_n - step, ctx_n) if arriving else me
            return pltpu.make_async_remote_copy(
                src_ref=source(peer), dst_ref=target.at[slot], send_sem=send.at[step],
                recv_sem=recv.at[slot], device_id={"ctx": peer}, device_id_type=MESH)
        return (lambda step: make(step, False)), (lambda step: make(step, True))

    out_a, in_a = over_ctx(lambda peer: msg.at[peer], got, sem_a, rsem_a)
    run(ctx_n, out_a)
    own = pltpu.make_async_copy(msg.at[me], got.at[me], local_sem.at[0])
    own.start()

    for tile in range(tiles):
        cols = pl.ds(tile * TILE, TILE)
        gated, dconv = gated_s[:, cols], dconv_s[:, cols]
        base = skip_ref[:, cols] * gated.astype(F32)
        for mode in range(modes):
            for kind in range(2):
                row = (2 * mode + kind) * block
                term = jnp.dot(dense[row : row + block, :], gated, preferred_element_type=F32)
                if kind == 0:
                    base = base + res_ref[mode : mode + 1, cols] * term
                slot = (mode // HALF) * 2 * HALF + kind * HALF + mode % HALF
                sums[slot : slot + 1, :] = jnp.sum(dconv * term, axis=0, keepdims=True)
        base_s[:, cols] = base
        totals = sums[...].astype(BF16)
        for group in range(TILE // LANES):
            cut = slice(group * LANES, (group + 1) * LANES)
            for half in range(2):
                slot = (TILE // LANES * tile + group) * 2 + half
                late[slot] = totals[half * 16 : half * 16 + 16, cut]

    out_f, in_f = over_ctx(lambda peer: late.at[peer], got_late, sem_f, rsem_f)
    run(ctx_n, out_f)
    own_late = pltpu.make_async_copy(late.at[me], got_late.at[me], local_sem.at[2])
    own_late.start()

    own_half = lax.rem(me, 2)
    own_group = me // 2
    first = pl.multiple_of(own_half * HALF, HALF)
    own_decay = rate_rows[pl.ds(first, HALF), :] * (-1.0 / seq_len)
    own_res = res_ref[pl.ds(first, HALF), pl.ds(pl.multiple_of(own_group * LANES, LANES), LANES)]
    own_number = (lax.broadcasted_iota(jnp.int32, (HALF, LANES), 0) + (own_half * HALF + 1)).astype(F32)

    def turn(steps):
        size = jnp.exp(own_decay * steps)
        angle = wave_angle(own_number * steps)
        return size * jnp.cos(angle), size * jnp.sin(angle)

    turn_c, turn_s = turn(float(block))
    last_c, last_s = turn(float(block * (ctx_n - 2)))
    step_len = 1.0 / ctx_n
    span = step_len * (ctx_n - 2)
    zero = jnp.zeros((HALF, LANES), F32)

    def states(index, start):
        pair = got[index, start : start + 16, :]
        return pair[:HALF], pair[HALF:]

    def times_turn(real, imag):
        return real * turn_c - imag * turn_s, real * turn_s + imag * turn_c

    def times_last(real, imag):
        return real * last_c - imag * last_s, real * last_s + imag * last_c

    def advance(index, carry):
        hr, hi, dr, di = carry
        ur, ui = states(index, 0)
        wr, wi = states(index, 16)
        nr, ni = times_turn(hr, hi)
        er, ei = times_turn(dr + step_len * hr, di + step_len * hi)
        return nr + ur, ni + ui, er + wr, ei + wi

    own.wait()
    land(ctx_n, in_a)
    carry = (zero, zero, zero, zero)
    for index in range(1, ctx_n):
        carry = advance(index, carry)
    gsum, dsum = zero, zero
    for index in range(ctx_n):
        hr, hi, dr, di = carry
        backs[index] = jnp.concatenate([hr, hi], axis=0).astype(BF16)
        vr, vi = states(index, 32)
        xr, xi = states(index, 48)
        gsum = gsum + (vr * hr - vi * hi)
        dsum = dsum - ((xr * hr - xi * hi) + (vr * dr - vi * di))
        if index < ctx_n - 1:
            ur, ui = states(index + 1, 0)
            wr, wi = states(index + 1, 16)
            lr, li = times_last(ur, ui)
            pr, pi_ = times_last(wr + span * ur, wi + span * ui)
            carry = advance(index, (hr - lr, hi - li, dr - pr, di - pi_))

    out_b, in_b = over_ctx(lambda peer: backs.at[peer], state, sem_b, rsem_b)
    run(ctx_n, out_b)
    mine = pltpu.make_async_copy(backs.at[me], state.at[me], local_sem.at[1])
    mine.start()
    own_late.wait()
    land(ctx_n, in_f)
    for index in range(ctx_n):
        pair = got_late[index].astype(F32)
        gsum = gsum + pair[:HALF]
        dsum = dsum + pair[HALF:]
    rate = jnp.broadcast_to(jnp.sum(dsum * own_res, axis=1, keepdims=True), (HALF, LANES))
    rate_u, rate_l = halves(rate)
    left_half = lax.broadcasted_iota(jnp.int32, (HALF, LANES), 1) < LANES // 2
    rate = jnp.where(left_half, rate_u.astype(F32), rate_l.astype(F32))
    parts[rank] = jnp.concatenate([gsum, rate], axis=0).astype(BF16)

    def over_dp(arriving):
        def make(step):
            peer = lax.rem(rank + step, dp_n)
            slot = lax.rem(rank + dp_n - step, dp_n) if arriving else rank
            return pltpu.make_async_remote_copy(
                src_ref=parts.at[rank], dst_ref=parts.at[slot], send_sem=sem_c.at[step],
                recv_sem=rsem_c.at[slot], device_id={"dp": peer}, device_id_type=MESH)
        return make

    run(dp_n, over_dp(False))
    mine.wait()
    land(ctx_n, in_b)

    for tile in range(tiles):
        cols = pl.ds(tile * TILE, TILE)
        pieces = []
        for group in range(TILE // LANES):
            slot = (TILE // LANES * tile + group) * 2
            pieces.append(jnp.concatenate(
                [state[slot].astype(F32), state[slot + 1].astype(F32)], axis=0))
        low, high = res_ref[0:HALF, cols], res_ref[HALF : 2 * HALF, cols]
        weight = jnp.concatenate([low, low, high, high], axis=0)
        scaled = (jnp.concatenate(pieces, axis=1) * weight).astype(BF16)
        conv = jnp.dot(spread[:, : 2 * modes], scaled, preferred_element_type=F32)
        out_ref[cols, :] = (query_s[:, cols] * (base_s[:, cols] + conv)).T.astype(BF16)

    put = pltpu.make_async_copy(out_ref, out_hbm, local_sem.at[0])
    put.start()
    land(dp_n, over_dp(True))
    total = parts[0].astype(F32)
    for index in range(1, dp_n):
        total = total + parts[index].astype(F32)
    grads[me] = total
    out_e, in_e = over_ctx(lambda peer: grads.at[me], grads, sem_e, rsem_e)
    run(ctx_n, out_e)
    left(ctx_n, out_a)
    left(ctx_n, out_b)
    left(ctx_n, out_f)
    put.wait()
    left(dp_n, over_dp(False))
    land(ctx_n, in_e)
    for half in range(2):
        rate = zero
        for group in range(ctx_n // 2):
            piece = grads[group * 2 + half]
            gres_ref[half * HALF : (half + 1) * HALF, group * LANES : (group + 1) * LANES] = piece[:HALF]
            rate = rate + piece[HALF:]
        rate = jnp.sum(rate, axis=1, keepdims=True) * (2.0 / LANES)
        grate_ref[half * HALF : (half + 1) * HALF, :] = jnp.broadcast_to(rate, (HALF, LANES))
    left(ctx_n, out_e)


def per_device(dp_n, token_ids, feature_table, short_weight, residue, rates, skip_gain, grad_out):
    block = token_ids.shape[1]
    ctx_n = lax.axis_size("ctx")
    channels, modes = residue.shape
    vocab = feature_table.shape[1]
    taps = short_weight.shape[1]

    dma = pltpu.SemaphoreType.DMA
    vmem = pl.BlockSpec(memory_space=pltpu.VMEM)
    hbm = pl.BlockSpec(memory_space=pltpu.HBM)
    previous = pl.pallas_call(
        functools.partial(ids_kernel, ctx_n),
        in_specs=[vmem],
        out_specs=vmem,
        out_shape=jax.ShapeDtypeStruct(token_ids.shape, token_ids.dtype),
        scratch_shapes=[dma, dma],
        compiler_params=pltpu.CompilerParams(collective_id=1, has_side_effects=True),
    )(token_ids)
    mixed, grad_res, grad_rate = pl.pallas_call(
        functools.partial(layer_kernel, ctx_n, dp_n),
        in_specs=[pl.BlockSpec(memory_space=pltpu.SMEM)] + [hbm] * 7,
        out_specs=[hbm, vmem, vmem],
        out_shape=[jax.ShapeDtypeStruct((channels, block), BF16),
                   jax.ShapeDtypeStruct((modes, channels), F32),
                   jax.ShapeDtypeStruct((modes, LANES), F32)],
        scratch_shapes=[
            pltpu.VMEM(token_ids.shape, jnp.int32),
            pltpu.VMEM(token_ids.shape, jnp.int32),
            pltpu.VMEM((taps, 3 * channels), F32),
            pltpu.VMEM((modes, channels), F32),
            pltpu.VMEM((1, channels), F32),
            pltpu.VMEM((channels, block), BF16),
            pltpu.VMEM((block, channels), BF16),
            pltpu.VMEM((block, channels), F32),
            pltpu.VMEM((ctx_n, 16, LANES), BF16),
            pltpu.VMEM((ctx_n, 16, LANES), BF16),
            pltpu.VMEM((3, channels, vocab), BF16),
            pltpu.VMEM((channels, block), BF16),
            pltpu.VMEM((2 * modes * block, block), BF16),
            pltpu.VMEM((4 * modes, block), F32),
            pltpu.VMEM((4 * modes, block), F32),
            pltpu.VMEM((block, block), BF16),
            pltpu.VMEM((modes, LANES), F32),
            pltpu.VMEM((3, block + 8, TILE), F32),
            pltpu.VMEM((2 * modes, TILE), F32),
            pltpu.VMEM((block, channels), F32),
            pltpu.VMEM((block, channels), F32),
            pltpu.VMEM((ctx_n, 64, LANES), F32),
            pltpu.VMEM((ctx_n, 64, LANES), F32),
            pltpu.VMEM((ctx_n, 16, LANES), BF16),
            pltpu.VMEM((ctx_n, 16, LANES), BF16),
            pltpu.VMEM((dp_n, 16, LANES), BF16),
            pltpu.VMEM((ctx_n, 16, LANES), F32),
            dma((ctx_n,)), dma((ctx_n,)), dma((dp_n,)), dma((ctx_n,)), dma((ctx_n,)),
            dma((ctx_n,)), dma((ctx_n,)), dma((dp_n,)), dma((ctx_n,)), dma((ctx_n,)),
            dma((channels // TILE + 6,)),
        ],
        compiler_params=pltpu.CompilerParams(
            collective_id=0, has_side_effects=True, vmem_limit_bytes=67043328),
    )(rates, token_ids, previous, short_weight.T, residue.T, skip_gain[None, :],
      feature_table.reshape(3, channels, vocab), grad_out[0])
    return (mixed[None], grad_res.T, grad_rate[:, 0])


def solution(mesh):
    return jax.shard_map(
        functools.partial(per_device, mesh.shape["dp"]),
        mesh=mesh,
        in_specs=(P("dp", "ctx"), P(), P(), P(), P(), P(), P("dp", None, "ctx")),
        out_specs=(P("dp", None, "ctx"), P(), P()),
        check_vma=False,
    )
```

time: 721 us -> 57 us (0.08)
  waiting for transfers between devices: 407 us -> 0 us
  blocking collectives: 109 us -> 0 us
  matrix products: 94.2 us -> 0 us
  Pallas kernels: 0 us -> 51.6 us
  starting transfers between devices: 33.8 us -> 0 us
  local copies, waits for them, and re-layouts: 31.4 us -> 4.46 us
  other arithmetic: 25.3 us -> 0 us
  between operations: 14.4 us -> 0.65 us
    psum x1 -> x0, waiting for transfers between devices: 339 us -> none  [per_device(): grad_residue, grad_rate = lax.psum((grad_part, rate_part), ('ctx', 'dp'))]
    psum x1 -> x0, blocking collectives: 109 us -> none  [per_device(): grad_residue, grad_rate = lax.psum((grad_part, rate_part), ('ctx', 'dp'))]
    dot_general x84 -> x0, matrix products: 94.2 us -> none  [the longest x16 30 us: pair_terms(): filt_spec = jnp.dot(residue, spectra[:modes], precision=HIGHEST)]
    ppermute x16 -> x0, waiting for transfers between devices: 67.9 us -> none  [from_behind(): return lax.ppermute(block, axis, route)]
    pallas_call x0 -> x2, Pallas kernels: none -> 51.6 us  [the longest x1 42.2 us: per_device(): pl.pallas_call(functools.partial(layer_kernel, ctx_n, dp_n), in_specs=[pl...]
    ppermute x16 -> x0, starting transfers between devices: 33.8 us -> none  [from_behind(): return lax.ppermute(block, axis, route)]
    while x135 -> x0, local copies, waits for them, and re-layouts: 20.4 us -> none
    select_n x33 -> x0, other arithmetic: 10 us -> none  [the longest x16 9.3 us: packed_product(): jnp.where(leading, left_re * right_re, left_re * right_re + left_im * rig...]
  transfers between devices with their start and end apart: 17 -> 0, of which waited for: 16 -> 0; matrix products, arithmetic and copies ran while one was open for 9% -> 0% of each run, Pallas kernels for 0% -> 0%
where the time goes in v2:
time: 57 us; the launch traced here: 56.7 us
  Pallas kernels  51.6 us (91%)
  local copies, waits for them, and re-layouts  4.46 us (8%)
  between operations  0.65 us (1%)
    pallas_call x1, Pallas kernels, per_device(): pl.pallas_call(functools.partial(layer_kernel, ctx_n, dp_n), in_specs=[pl...  42.2 us
    pallas_call x1, Pallas kernels, per_device(): pl.pallas_call(functools.partial(ids_kernel, ctx_n), in_specs=[vmem], out...  9.36 us
    unnamed x2, local copies, waits for them, and re-layouts  3.14 us
    slice x1, local copies, waits for them, and re-layouts, per_device(): return (mixed[None], grad_res.T, grad_rate[:, 0])  1.32 us

profile of v2, /device:TPU:1, one launch (start us, length us, event | category | flops | bytes accessed | tf_op | source)
XLA Modules:
  0.0 56.7 jit_solution(12974002826930793869)
XLA Ops:
  0.6 9.4 %shard_map.94.prev_hbm = s32[1,128]{1,0:T(1,128)} custom-call(s32[1,128]{1,0:T(1,128)} %ids_hbm.1), custom_call_target="tpu_custom_call" | custom-call | tf_op jit(solution)/shard_map/pallas_call | solution.py:358
  10.0 42.2 %shard_map.95 = (bf16[1024,128]{1,0:T(8,128)(2,1)}, f32[16,1024]{1,0:T(8,128)}, f32[16,128]{1,0:T(8,128)}) custom-call(f32[16]{0:T(128)} %rates_ref.1, s32[1,128]{1,0:T(1,128)} %ids_hbm.1, s32[1,128]{1,0:T(1,128)} %shard_map.94.prev_hbm, f32[7,3072]{1,0:T(8,128)} %bitcast.10, f32[16,1024]{1,0:T(8,128)} %bitcast.11, f32[1,1024]{1,0:T(1,128)} %bitcast.13, ...), custom_call_target="tpu_custom_call" | custom-call | tf_op jit(solution)/shard_map/pallas_call | solution.py:366
  52.2 1.3 %slice_reduce_fusion = f32[16]{0:T(128)} fusion(f32[16,128]{1,0:T(8,128)} %get-tuple-element.8), kind=kLoop, calls=%fused_computation | loop fusion | bytes 128 | tf_op jit(solution)/shard_map/slice | solution.py:409
  53.6 1.7 %copy.12 = bf16[1,1024,128]{2,1,0:T(8,128)(2,1)} copy(bf16[1,1024,128]{2,1,0:T(8,128)(2,1)} %bitcast.9) | data formatting | bytes 524288
  55.2 1.5 %copy.13 = f32[1024,16]{0,1:T(8,128)} copy(f32[1024,16]{0,1:T(8,128)} %bitcast.12) | data formatting | bytes 131072

commit v3 on v2

--- a/solution.py
+++ b/solution.py
@@ -16,25 +16,12 @@
 LANES = 128
 
 
-def ids_kernel(ctx_n, ids_ref, prev_ref, send_sem, recv_sem):
-    me = lax.axis_index("ctx")
-    right, left = lax.rem(me + 1, ctx_n), lax.rem(me + ctx_n - 1, ctx_n)
-    barrier = pltpu.get_barrier_semaphore()
-    pl.semaphore_signal(barrier, inc=1, device_id={"ctx": left}, device_id_type=MESH)
-    pl.semaphore_wait(barrier, 1)
-    copy = pltpu.make_async_remote_copy(
-        src_ref=ids_ref, dst_ref=prev_ref, send_sem=send_sem, recv_sem=recv_sem,
-        device_id={"ctx": right}, device_id_type=MESH)
-    copy.start()
-    copy.wait()
-
-
-def layer_kernel(ctx_n, dp_n, rates_ref, ids_hbm, prev_hbm, short_hbm, res_hbm, skip_hbm, table_hbm, gout_hbm,
-                 out_hbm, gres_ref, grate_ref,
+def layer_kernel(ctx_n, dp_n, rates_ref, ids_hbm, short_hbm, res_hbm, skip_hbm, table_hbm, gout_hbm,
+                 out_hbm, grad_ref,
                  ids_ref, prev_ref, short_ref, res_ref, skip_ref, out_ref, gated_s, dconv_s, late, got_late,
                  table, gout, dense, into, onto, spread, rate_rows, feat, sums, query_s, base_s,
                  msg, got, backs, state, parts, grads,
-                 sem_a, sem_b, sem_c, sem_e, sem_f, rsem_a, rsem_b, rsem_c, rsem_e, rsem_f, local_sem):
+                 sem_a, sem_b, sem_c, sem_e, sem_f, ids_sem, rsem_a, rsem_b, rsem_c, rsem_e, rsem_f, local_sem):
     me = lax.axis_index("ctx")
     rank = lax.axis_index("dp")
     modes, channels = res_ref.shape
@@ -59,7 +46,7 @@
     lax.fori_loop(1, ctx_n, greet_ctx, 0)
 
     small = []
-    pairs = ((ids_hbm, ids_ref), (prev_hbm, prev_ref), (short_hbm, short_ref), (res_hbm, res_ref),
+    pairs = ((ids_hbm, ids_ref), (short_hbm, short_ref), (res_hbm, res_ref),
              (skip_hbm, skip_ref), (gout_hbm, gout))
     for index, (source, target) in enumerate(pairs):
         small.append(pltpu.make_async_copy(source, target, local_sem.at[tiles + index]))
@@ -70,6 +57,8 @@
         loads.append(pltpu.make_async_copy(table_hbm.at[:, part], table.at[:, part], local_sem.at[tile]))
         loads[-1].start()
 
+    grad_ref[...] = jnp.zeros_like(grad_ref)
+
     def wave_angle(product):
         turns = jnp.floor(product * (1.0 / period))
         return (product - period * turns) * (2.0 * math.pi / period)
@@ -113,6 +102,13 @@
 
     for copy in small:
         copy.wait()
+    pl.semaphore_wait(barrier, ctx_n - 1 + dp_n - 1)
+    pass_ids = pltpu.make_async_remote_copy(
+        src_ref=ids_ref, dst_ref=prev_ref, send_sem=ids_sem.at[0], recv_sem=ids_sem.at[1],
+        device_id={"ctx": lax.rem(me + 1, ctx_n)}, device_id_type=MESH)
+    pass_ids.start()
+    lax.fori_loop(0, modes, fill_dense, (jnp.ones((block, block), F32), base_wave))
+    pass_ids.wait()
 
     def spell(ref):
         square = jnp.broadcast_to(ref[...].astype(F32), (block, block)).T
@@ -161,9 +157,6 @@
                 msg[slot, 0:32, :] = upper[half * 32 : half * 32 + 32, cut]
                 msg[slot, 32:64, :] = lower[half * 32 : half * 32 + 32, cut]
 
-    lax.fori_loop(0, modes, fill_dense, (jnp.ones((block, block), F32), base_wave))
-    pl.semaphore_wait(barrier, ctx_n - 1 + dp_n - 1)
-
     def run(count, make):
         def body(step, carry):
             make(step).start()
@@ -201,9 +194,10 @@
         gated, dconv = gated_s[:, cols], dconv_s[:, cols]
         base = skip_ref[:, cols] * gated.astype(F32)
         for mode in range(modes):
+            row = 2 * mode * block
+            both = jnp.dot(dense[row : row + 2 * block, :], gated, preferred_element_type=F32)
             for kind in range(2):
-                row = (2 * mode + kind) * block
-                term = jnp.dot(dense[row : row + block, :], gated, preferred_element_type=F32)
+                term = both[kind * block : (kind + 1) * block]
                 if kind == 0:
                     base = base + res_ref[mode : mode + 1, cols] * term
                 slot = (mode // HALF) * 2 * HALF + kind * HALF + mode % HALF
@@ -331,6 +325,7 @@
     left(ctx_n, out_a)
     left(ctx_n, out_b)
     left(ctx_n, out_f)
+    line = jnp.zeros((1, LANES), F32)
     put.wait()
     left(dp_n, over_dp(False))
     land(ctx_n, in_e)
@@ -338,10 +333,13 @@
         rate = zero
         for group in range(ctx_n // 2):
             piece = grads[group * 2 + half]
-            gres_ref[half * HALF : (half + 1) * HALF, group * LANES : (group + 1) * LANES] = piece[:HALF]
+            grad_ref[half * HALF : (half + 1) * HALF, group * LANES : (group + 1) * LANES] = piece[:HALF]
             rate = rate + piece[HALF:]
         rate = jnp.sum(rate, axis=1, keepdims=True) * (2.0 / LANES)
-        grate_ref[half * HALF : (half + 1) * HALF, :] = jnp.broadcast_to(rate, (HALF, LANES))
+        spot = lax.broadcasted_iota(jnp.int32, (HALF, LANES), 1)
+        spot = spot == lax.broadcasted_iota(jnp.int32, (HALF, LANES), 0) + half * HALF
+        line = line + jnp.sum(jnp.where(spot, rate, 0.0), axis=0, keepdims=True)
+    grad_ref[modes : modes + 1, 0:LANES] = line
     left(ctx_n, out_e)
 
 
@@ -355,21 +353,12 @@
     dma = pltpu.SemaphoreType.DMA
     vmem = pl.BlockSpec(memory_space=pltpu.VMEM)
     hbm = pl.BlockSpec(memory_space=pltpu.HBM)
-    previous = pl.pallas_call(
-        functools.partial(ids_kernel, ctx_n),
-        in_specs=[vmem],
-        out_specs=vmem,
-        out_shape=jax.ShapeDtypeStruct(token_ids.shape, token_ids.dtype),
-        scratch_shapes=[dma, dma],
-        compiler_params=pltpu.CompilerParams(collective_id=1, has_side_effects=True),
-    )(token_ids)
-    mixed, grad_res, grad_rate = pl.pallas_call(
+    mixed, grads = pl.pallas_call(
         functools.partial(layer_kernel, ctx_n, dp_n),
-        in_specs=[pl.BlockSpec(memory_space=pltpu.SMEM)] + [hbm] * 7,
-        out_specs=[hbm, vmem, vmem],
+        in_specs=[pl.BlockSpec(memory_space=pltpu.SMEM)] + [hbm] * 6,
+        out_specs=[hbm, vmem],
         out_shape=[jax.ShapeDtypeStruct((channels, block), BF16),
-                   jax.ShapeDtypeStruct((modes, channels), F32),
-                   jax.ShapeDtypeStruct((modes, LANES), F32)],
+                   jax.ShapeDtypeStruct((modes + 8, channels), F32)],
         scratch_shapes=[
             pltpu.VMEM(token_ids.shape, jnp.int32),
             pltpu.VMEM(token_ids.shape, jnp.int32),
@@ -398,15 +387,15 @@
             pltpu.VMEM((ctx_n, 16, LANES), BF16),
             pltpu.VMEM((dp_n, 16, LANES), BF16),
             pltpu.VMEM((ctx_n, 16, LANES), F32),
+            dma((ctx_n,)), dma((ctx_n,)), dma((dp_n,)), dma((ctx_n,)), dma((ctx_n,)), dma((2,)),
             dma((ctx_n,)), dma((ctx_n,)), dma((dp_n,)), dma((ctx_n,)), dma((ctx_n,)),
-            dma((ctx_n,)), dma((ctx_n,)), dma((dp_n,)), dma((ctx_n,)), dma((ctx_n,)),
-            dma((channels // TILE + 6,)),
+            dma((channels // TILE + 5,)),
         ],
         compiler_params=pltpu.CompilerParams(
             collective_id=0, has_side_effects=True, vmem_limit_bytes=67043328),
-    )(rates, token_ids, previous, short_weight.T, residue.T, skip_gain[None, :],
+    )(rates, token_ids, short_weight.T, residue.T, skip_gain[None, :],
       feature_table.reshape(3, channels, vocab), grad_out[0])
-    return (mixed[None], grad_res.T, grad_rate[:, 0])
+    return (mixed[None], grads[:modes].T, grads[modes, :modes])
 
 
 def solution(mesh):

time: 57 us -> 55.5 us (0.974)
  Pallas kernels: 51.6 us -> 50.3 us
    pallas_call x1 -> x0, Pallas kernels: 9.36 us -> none  [per_device(): pl.pallas_call(functools.partial(ids_kernel, ctx_n), in_specs=[vmem], out...]
    pallas_call x1, Pallas kernels: 42.2 us -> 50.3 us  [per_device(): pl.pallas_call(functools.partial(layer_kernel, ctx_n, dp_n), in_specs=[pl...]
    transpose x0 -> x1, local copies, waits for them, and re-layouts: none -> 1.47 us  [per_device(): return (mixed[None], grads[:modes].T, grads[modes, :modes])]
    unnamed x2 -> x1, local copies, waits for them, and re-layouts: 3.14 us -> 1.67 us
    slice x1 -> x0, local copies, waits for them, and re-layouts: 1.32 us -> none  [per_device(): return (mixed[None], grad_res.T, grad_rate[:, 0])]
    squeeze x0 -> x1, local copies, waits for them, and re-layouts: none -> 1.19 us  [per_device(): return (mixed[None], grads[:modes].T, grads[modes, :modes])]
where the time goes in v3:
time: 55.5 us; the launch traced here: 55.2 us
  Pallas kernels  50.3 us (91%)
  local copies, waits for them, and re-layouts  4.33 us (8%)
  between operations  0.64 us (1%)
    pallas_call x1, Pallas kernels, per_device(): pl.pallas_call(functools.partial(layer_kernel, ctx_n, dp_n), in_specs=[pl...  50.3 us
    unnamed x1, local copies, waits for them, and re-layouts  1.67 us
    transpose x1, local copies, waits for them, and re-layouts, per_device(): return (mixed[None], grads[:modes].T, grads[modes, :modes])  1.47 us
    squeeze x1, local copies, waits for them, and re-layouts, per_device(): return (mixed[None], grads[:modes].T, grads[modes, :modes])  1.19 us

profile of v3, /device:TPU:1, one launch (start us, length us, event | category | flops | bytes accessed | tf_op | source)
XLA Modules:
  0.0 55.2 jit_solution(17737657623824834622)
XLA Ops:
  0.6 50.3 %shard_map.94 = (bf16[1024,128]{1,0:T(8,128)(2,1)}, f32[24,1024]{1,0:T(8,128)}) custom-call(f32[16]{0:T(128)} %rates_ref.1, s32[1,128]{1,0:T(1,128)} %ids_hbm.1, f32[7,3072]{1,0:T(8,128)} %bitcast.13, f32[16,1024]{1,0:T(8,128)} %bitcast.14, f32[1,1024]{1,0:T(1,128)} %bitcast.15, bf16[3,1024,512]{2,1,0:T(8,128)(2,1)} %bitcast.10, bf16[1024,128]{1,0:T(8,128)(2,1)} %bitcast.11), custom_call_target="tpu_custom_call" | custom-call | tf_op jit(solution)/shard_map/pallas_call | solution.py:356
  50.9 1.5 %slice_bitcast_fusion = f32[1024,16]{0,1:T(8,128)} fusion(f32[24,1024]{1,0:T(8,128)} %get-tuple-element.6), kind=kLoop, calls=%fused_computation | loop fusion | bytes 131072 | tf_op jit(solution)/shard_map/transpose | solution.py:398
  52.4 1.2 %slice_bitcast_fusion.1 = f32[16]{0:T(128)} fusion(f32[24,1024]{1,0:T(8,128)} %get-tuple-element.6), kind=kLoop, calls=%fused_computation.1 | loop fusion | bytes 128 | tf_op jit(solution)/shard_map/squeeze | solution.py:398
  53.6 1.7 %copy.11 = bf16[1,1024,128]{2,1,0:T(8,128)(2,1)} copy(bf16[1,1024,128]{2,1,0:T(8,128)(2,1)} %bitcast.12) | data formatting | bytes 524288

commit v4 on v3

--- a/solution.py
+++ b/solution.py
@@ -52,8 +52,13 @@
         small.append(pltpu.make_async_copy(source, target, local_sem.at[tiles + index]))
         small[-1].start()
     loads = []
+    owners = 2 * TILE // LANES
+
+    def spin(index):
+        return lax.rem(me // owners + index, tiles)
+
     for tile in range(tiles):
-        part = pl.ds(tile * TILE, TILE)
+        part = pl.ds(pl.multiple_of(spin(tile) * TILE, TILE), TILE)
         loads.append(pltpu.make_async_copy(table_hbm.at[:, part], table.at[:, part], local_sem.at[tile]))
         loads[-1].start()
 
@@ -126,15 +131,45 @@
     onto_b = jnp.concatenate(halves(onto[...]), axis=0)
     states_n = 4 * modes
 
-    for tile in range(tiles):
-        loads[tile].wait()
-        at = tile * TILE
+    def run(count, make):
+        def body(step, carry):
+            make(step).start()
+            return carry
+        lax.fori_loop(1, count, body, 0)
+
+    def land(count, make):
+        def body(step, carry):
+            make(step).wait_recv()
+            return carry
+        lax.fori_loop(1, count, body, 0)
+
+    def left(count, make):
+        def body(step, carry):
+            make(step).wait_send()
+            return carry
+        lax.fori_loop(1, count, body, 0)
+
+    def over_ctx(source, target, send, recv):
+        def make(step, arriving):
+            peer = lax.rem(me + step, ctx_n)
+            slot = lax.rem(me + ctx_n - step, ctx_n) if arriving else me
+            return pltpu.make_async_remote_copy(
+                src_ref=source(peer), dst_ref=target.at[slot], send_sem=send.at[step],
+                recv_sem=recv.at[slot], device_id={"ctx": peer}, device_id_type=MESH)
+        return (lambda step: make(step, False)), (lambda step: make(step, True))
+
+    out_a, in_a = over_ctx(lambda peer: msg.at[peer], got, sem_a, rsem_a)
+
+    for turn_at in range(tiles):
+        loads[turn_at].wait()
+        tile = spin(turn_at)
+        at = pl.multiple_of(tile * TILE, TILE)
         cols = pl.ds(at, TILE)
         mixed = []
         for part in range(3):
             feat[part] = lax.dot_general(
                 onehot, table[part, cols, :], (((1,), (1,)), ((), ())), preferred_element_type=F32)
-            wide = pl.ds(part * channels + at, TILE)
+            wide = pl.ds(pl.multiple_of(part * channels + at, TILE), TILE)
             total = short_ref[0:1, wide] * feat[part, 2 : 2 + block, :]
             for tap in range(1, taps):
                 total = total + short_ref[tap : tap + 1, wide] * feat[part, 2 + tap : 2 + tap + block, :]
@@ -156,36 +191,13 @@
                 slot = (TILE // LANES * tile + group) * 2 + half
                 msg[slot, 0:32, :] = upper[half * 32 : half * 32 + 32, cut]
                 msg[slot, 32:64, :] = lower[half * 32 : half * 32 + 32, cut]
-
-    def run(count, make):
-        def body(step, carry):
-            make(step).start()
-            return carry
-        lax.fori_loop(1, count, body, 0)
-
-    def land(count, make):
-        def body(step, carry):
-            make(step).wait_recv()
-            return carry
-        lax.fori_loop(1, count, body, 0)
-
-    def left(count, make):
-        def body(step, carry):
-            make(step).wait_send()
-            return carry
-        lax.fori_loop(1, count, body, 0)
-
-    def over_ctx(source, target, send, recv):
-        def make(step, arriving):
-            peer = lax.rem(me + step, ctx_n)
-            slot = lax.rem(me + ctx_n - step, ctx_n) if arriving else me
-            return pltpu.make_async_remote_copy(
-                src_ref=source(peer), dst_ref=target.at[slot], send_sem=send.at[step],
-                recv_sem=recv.at[slot], device_id={"ctx": peer}, device_id_type=MESH)
-        return (lambda step: make(step, False)), (lambda step: make(step, True))
-
-    out_a, in_a = over_ctx(lambda peer: msg.at[peer], got, sem_a, rsem_a)
-    run(ctx_n, out_a)
+        for index in range(owners):
+            away = lax.rem(tile * owners + lax.rem(index + me, owners) + ctx_n - me, ctx_n)
+
+            @pl.when(away != 0)
+            def _():
+                out_a(away).start()
+
     own = pltpu.make_async_copy(msg.at[me], got.at[me], local_sem.at[0])
     own.start()
 

time: 55.5 us -> 54.4 us (0.980)
  Pallas kernels: 50.3 us -> 49.2 us
    pallas_call x1, Pallas kernels: 50.3 us -> 49.2 us  [per_device(): pl.pallas_call(functools.partial(layer_kernel, ctx_n, dp_n), in_specs=[pl...]
where the time goes in v4:
time: 54.4 us; the launch traced here: 54.2 us
  Pallas kernels  49.2 us (90%)
  local copies, waits for them, and re-layouts  4.33 us (8%)
  between operations  0.64 us (1%)
    pallas_call x1, Pallas kernels, per_device(): pl.pallas_call(functools.partial(layer_kernel, ctx_n, dp_n), in_specs=[pl...  49.2 us
    unnamed x1, local copies, waits for them, and re-layouts  1.67 us
    transpose x1, local copies, waits for them, and re-layouts, per_device(): return (mixed[None], grads[:modes].T, grads[modes, :modes])  1.47 us
    squeeze x1, local copies, waits for them, and re-layouts, per_device(): return (mixed[None], grads[:modes].T, grads[modes, :modes])  1.19 us

profile of v4, /device:TPU:1, one launch (start us, length us, event | category | flops | bytes accessed | tf_op | source)
XLA Modules:
  0.0 54.2 jit_solution(2231965565508420363)
XLA Ops:
  0.6 49.2 %shard_map.94 = (bf16[1024,128]{1,0:T(8,128)(2,1)}, f32[24,1024]{1,0:T(8,128)}) custom-call(f32[16]{0:T(128)} %rates_ref.1, s32[1,128]{1,0:T(1,128)} %ids_hbm.1, f32[7,3072]{1,0:T(8,128)} %bitcast.13, f32[16,1024]{1,0:T(8,128)} %bitcast.14, f32[1,1024]{1,0:T(1,128)} %bitcast.15, bf16[3,1024,512]{2,1,0:T(8,128)(2,1)} %bitcast.10, bf16[1024,128]{1,0:T(8,128)(2,1)} %bitcast.11), custom_call_target="tpu_custom_call" | custom-call | tf_op jit(solution)/shard_map/pallas_call | solution.py:368
  49.8 1.5 %slice_bitcast_fusion = f32[1024,16]{0,1:T(8,128)} fusion(f32[24,1024]{1,0:T(8,128)} %get-tuple-element.6), kind=kLoop, calls=%fused_computation | loop fusion | bytes 131072 | tf_op jit(solution)/shard_map/transpose | solution.py:410
  51.3 1.2 %slice_bitcast_fusion.1 = f32[16]{0:T(128)} fusion(f32[24,1024]{1,0:T(8,128)} %get-tuple-element.6), kind=kLoop, calls=%fused_computation.1 | loop fusion | bytes 128 | tf_op jit(solution)/shard_map/squeeze | solution.py:410
  52.5 1.7 %copy.11 = bf16[1,1024,128]{2,1,0:T(8,128)(2,1)} copy(bf16[1,1024,128]{2,1,0:T(8,128)(2,1)} %bitcast.12) | data formatting | bytes 524288
